TPU v7x, 32 devices: a whole 2x2x4 slice. The times are simulated.
32 devices in a mesh: gx: 2 (over y), gy: 4 (over x, core), gz: 4 (over z).
Axes of the slice: x: 2, y: 2, z: 4, core: 2. Of those that a mesh axis runs over, the one named last changes fastest.
Arguments:
- wavefunctions: bfloat16 [32, 64, 64, 128], P('gx', 'gy', 'gz'), may hold values from -512 to 512, as said below
- potential: float32 [32, 64, 64], P('gx', 'gy', 'gz'), may hold values from 0 to 3
Outputs:
- rotated: float32 [32, 64, 64, 128], P('gx', 'gy', 'gz')
- residual: bfloat16 [32, 64, 64, 128], P('gx', 'gy', 'gz')
- quotients: float32 [128], replicated
- norms: float32 [128], replicated
Inputs may be any that keep to these rules, and one draw needn't show every extreme that they name: `wavefunctions`: real values mixed across bands, of full rank.
All inputs are finite; a program needn't handle non-finite values.
Results may differ from a plain program's by a relative error of at most 0.0007.
Values may be sent and summed in bfloat16 or wider, within the bound.
A program may use at most 64 MiB of HBM per device.

v0:
```python
import jax
import jax.numpy as jnp
from jax import lax
from jax.sharding import PartitionSpec as P


def extended(block, sides, width):
    for axis, dim in sides:
        count = lax.axis_size(axis)
        forward = [(i, i + 1) for i in range(count - 1)]
        forward.append((count - 1, 0))
        backward = [(target, source) for source, target in forward]
        low = lax.ppermute(
            lax.slice_in_dim(block, block.shape[dim] - width, None, axis=dim), axis, forward
        )
        high = lax.ppermute(lax.slice_in_dim(block, 0, width, axis=dim), axis, backward)
        block = jnp.concatenate([low, block, high], axis=dim)
    return block


def stencil(padded, center, potential):
    cx, cy, cz = (center.shape[0], center.shape[1], center.shape[2])
    total = -30.0 * 3.0 * center
    weights = ((0, -1.0), (1, 16.0), (3, 16.0), (4, -1.0))
    for offset, weight in weights:
        total = total + weight * padded[offset : offset + cx, 2 : 2 + cy, 2 : 2 + cz]
        total = total + weight * padded[2 : 2 + cx, offset : offset + cy, 2 : 2 + cz]
        total = total + weight * padded[2 : 2 + cx, 2 : 2 + cy, offset : offset + cz]
    return -0.5 * total / 12.0 + potential[..., None] * center


def rotate(field, inverse):
    shape = field.shape
    flat = field.reshape(-1, shape[3])
    return jnp.dot(flat, inverse.T, precision=lax.Precision.HIGHEST).reshape(shape)


def local(wavefunctions, potential):
    cx, cy, cz, bands = wavefunctions.shape
    total_cells = cx * cy * cz * lax.axis_size("gx") * lax.axis_size("gy") * lax.axis_size("gz")
    flat = wavefunctions.reshape(-1, bands)
    local_correlation = lax.dot_general(
        flat, flat, (((0,), (0,)), ((), ())), preferred_element_type=jnp.float32
    )
    correlation = lax.psum(local_correlation, ("gx", "gy", "gz")) / total_cells
    factor = jnp.linalg.cholesky(correlation)
    inverse = lax.linalg.triangular_solve(
        factor, jnp.eye(bands, dtype=jnp.float32), left_side=True, lower=True
    )
    given = wavefunctions.astype(jnp.float32)
    rotated = rotate(given, inverse)
    padded = extended(rotated, (("gx", 0), ("gy", 1), ("gz", 2)), 2)
    applied = stencil(padded, rotated, potential)
    cross = jnp.sum(rotated * applied, axis=(0, 1, 2))
    self_applied = jnp.sum(applied * applied, axis=(0, 1, 2))
    self_rotated = jnp.sum(rotated * rotated, axis=(0, 1, 2))
    cross_all, applied_all, rotated_all = lax.psum(
        (cross, self_applied, self_rotated), ("gx", "gy", "gz")
    )
    quotients = cross_all / total_cells
    squares = applied_all - 2.0 * quotients * cross_all + quotients * quotients * rotated_all
    leftover = applied - quotients * rotated
    norms = jnp.sqrt(squares / total_cells + 1e-06)
    return (rotated, leftover.astype(jnp.bfloat16), quotients, norms)


def solution(mesh):
    placed = (P("gx", "gy", "gz", None), P("gx", "gy", "gz"))
    return jax.shard_map(
        local,
        mesh=mesh,
        in_specs=placed,
        out_specs=(P("gx", "gy", "gz", None), P("gx", "gy", "gz", None), P(), P()),
        check_vma=False,
    )
```

profile of v0, /device:TPU:0, one launch (start us, length us, event | category | flops | bytes accessed | tf_op | source)
XLA Modules:
  0.0 271.0 jit_solution(13407734252116796372)
XLA Ops:
  7.2 1.2 copy-done
  8.4 1.1 convolution_bitcast_fusion.1
  9.5 126.7 %all-reduce.3.cloned.1.call-done = f32[128,128]{0,1:T(8,128)} async-done(((f32[128,128]{0,1:T(8,128)}), f32[128,128]{0,1:T(8,128)}) %all-reduce.3.cloned.1.call-update) | async-done | bytes 65552 | tf_op jit(solution)/shard_map/psum | solution.py:45
  136.3 0.8 broadcast_multiply_fusion
  137.2 0.9 fusion.25
  138.1 11.7 %cholesky.17 = f32[128,128]{1,0:T(8,128)S(1)} custom-call(f32[128,128]{1,0:T(8,128)S(1)} %fusion.25), custom_call_target="Cholesky" | custom-call | tf_op jit(solution)/shard_map/jit(cholesky)/cholesky | solution.py:46
  149.8 0.6 compare_reduce_fusion
  150.5 0.7 fusion.22
  151.1 9.8 %custom-call.6 = f32[1,128,128]{1,2,0:T(8,128)S(1)} custom-call(f32[1,128,128]{2,1,0:T(8,128)S(1)} %fusion.22), custom_call_target="InvertDiagBlocksLowerTriangular" | custom-call | tf_op jit(solution)/shard_map/triangular_solve | solution.py:47
  161.2 1.1 multiply_reduce_fusion
  162.3 1.3 copy-done.2
  163.7 0.8 copy.21
  164.5 0.8 copy.22
  165.3 1.5 collective-permute-start.1
  166.8 0.6 collective-permute-start
  167.4 1.9 copy.20
  169.3 4.7 %collective-permute-done.1 = f32[2,16,16,128]{3,2,1,0:T(8,128)S(1)} collective-permute-done((f32[2,16,16,128]{3,2,1,0:T(8,128)}, f32[2,16,16,128]{3,2,1,0:T(8,128)S(1)}, u32[]{:S(2)}, u32[]{:S(2)}) %collective-permute-start.1) | collective-permute-done | bytes 262176 | tf_op jit(solution)/shard_map/ppermute | solution.py:16
  174.0 5.7 %collective-permute-done = f32[2,16,16,128]{3,2,1,0:T(8,128)} collective-permute-done((f32[2,16,16,128]{3,2,1,0:T(8,128)}, f32[2,16,16,128]{3,2,1,0:T(8,128)}, u32[]{:S(2)}, u32[]{:S(2)}) %collective-permute-start) | collective-permute-done | bytes 262176 | tf_op jit(solution)/shard_map/ppermute | solution.py:13
  179.7 0.8 pad_maximum_fusion.20
  180.5 0.6 collective-permute-start.2
  181.2 1.2 collective-permute-start.3
  182.3 6.5 %collective-permute-done.2 = f32[20,2,16,128]{3,2,1,0:T(8,128)S(1)} collective-permute-done((f32[20,2,16,128]{3,2,1,0:T(8,128)S(1)}, f32[20,2,16,128]{3,2,1,0:T(8,128)S(1)}, u32[]{:S(2)}, u32[]{:S(2)}) %collective-permute-start.2) | collective-permute-done | bytes 327712 | tf_op jit(solution)/shard_map/ppermute | solution.py:13
  188.8 0.7 collective-permute-done.3
  189.6 1.3 pad_maximum_fusion.17
  190.8 1.2 collective-permute-start.4
  192.0 2.7 %collective-permute-start.5 = (f32[20,20,2,128]{3,2,1,0:T(2,128)S(1)}, f32[20,20,2,128]{3,2,1,0:T(2,128)S(1)}, u32[]{:S(2)}, u32[]{:S(2)}) collective-permute-start(f32[20,20,2,128]{3,2,1,0:T(2,128)S(1)} %get-tuple-element.17), channel_id=1, source_target_pairs={{1,0},{2,1},{3,2},{0,3},{5,4},{6,5},{7,6},{4,7},{9,8},{10,9},{11,1... | collective-permute-start | bytes 1228808 | tf_op jit(solution)/shard_map/ppermute | solution.py:16
  194.7 1.6 maximum_maximum_fusion
  196.4 8.7 %collective-permute-done.4 = f32[20,20,2,128]{3,2,1,0:T(2,128)S(1)} collective-permute-done((f32[20,20,2,128]{3,2,1,0:T(2,128)S(1)}, f32[20,20,2,128]{3,2,1,0:T(2,128)S(1)}, u32[]{:S(2)}, u32[]{:S(2)}) %collective-permute-start.4) | collective-permute-done | bytes 409632 | tf_op jit(solution)/shard_map/ppermute | solution.py:13
  205.1 7.6 %collective-permute-done.5 = f32[20,20,2,128]{3,2,1,0:T(2,128)S(1)} collective-permute-done((f32[20,20,2,128]{3,2,1,0:T(2,128)S(1)}, f32[20,20,2,128]{3,2,1,0:T(2,128)S(1)}, u32[]{:S(2)}, u32[]{:S(2)}) %collective-permute-start.5) | collective-permute-done | bytes 409632 | tf_op jit(solution)/shard_map/ppermute | solution.py:16
  212.7 8.0 %multiply_reduce_fusion.1 = (f32[128]{0:T(128)S(1)}, f32[128]{0:T(128)S(1)}, f32[16,16,16,128]{3,2,1,0:T(8,128)}) fusion(f32[16,16,16,128]{3,2,1,0:T(8,128)S(1)} %bitcast.26, f32[16,16,16]{2,1,0:T(8,128)S(1)} %copy-done.3, f32[20,20,2,128]{3,2,1,0:T(2,128)S(1)} %collective-permute-done.5, f32[20,2,16,128]{3,2,1,0:T(8,128)S(1)} %collective-permute-done.3, ...), kind=kLoop, calls=%fused_computation.48 | loop fusion | flops 29359872 | bytes 14599168 | tf_op jit(solution)/shard_map/reduce_sum | solution.py:55
  220.7 40.1 %all-reduce = (f32[128]{0:T(128)S(1)}, f32[128]{0:T(128)S(1)}, f32[128]{0:T(128)S(1)}) all-reduce(f32[128]{0:T(128)S(1)} %get-tuple-element.9, f32[128]{0:T(128)S(1)} %get-tuple-element.24, f32[128]{0:T(128)S(1)} %get-tuple-element.8), channel_id=1, replica_groups=mesh['gx'=2,'gy'=4,'gz'=4] {'gx','gy','gz'}, use_global_device_ids=true, to_apply=%region_4.5 | all-reduce | flops 384 | bytes 3072 | tf_op jit(solution)/shard_map/psum | solution.py:57
  261.3 2.8 %subtract_convert_fusion = bf16[16,16,16,128]{3,2,1,0:T(8,128)(2,1)} fusion(f32[16,16,16,128]{3,2,1,0:T(8,128)} %get-tuple-element.15, f32[128]{0:T(128)S(1)} %get-tuple-element.14, f32[4096,128]{1,0:T(8,128)S(1)} %copy.20), kind=kLoop, calls=%fused_computation.49 | loop fusion | flops 1572864 | bytes 5243392 | tf_op jit(solution)/shard_map/convert_element_type | solution.py:64
  (15 shorter events, 1.0 us)
Async XLA Ops:
  7.2 1.2 copy-start
  7.2 129.1 %all-reduce.3.cloned.1.call-start = ((), (), s32[]{:S(2)}) async-start(), calls=%async_computation | async-start | bytes 131072 | tf_op jit(solution)/shard_map/psum | solution.py:45
  162.3 1.3 copy-start.2
  165.3 8.6 %collective-permute-start.1 = (f32[2,16,16,128]{3,2,1,0:T(8,128)}, f32[2,16,16,128]{3,2,1,0:T(8,128)S(1)}, u32[]{:S(2)}, u32[]{:S(2)}) collective-permute-start(f32[2,16,16,128]{3,2,1,0:T(8,128)} %bitcast.8), channel_id=1, source_target_pairs={{16,0},{0,16},{17,1},{1,17},{18,2},{2,18},{19,3},{3,19},{20,4},{4,... | collective-permute-start | bytes 786440 | tf_op jit(solution)/shard_map/ppermute | solution.py:16
  166.8 12.9 %collective-permute-start = (f32[2,16,16,128]{3,2,1,0:T(8,128)}, f32[2,16,16,128]{3,2,1,0:T(8,128)}, u32[]{:S(2)}, u32[]{:S(2)}) collective-permute-start(f32[2,16,16,128]{3,2,1,0:T(8,128)} %bitcast.7), channel_id=1, source_target_pairs={{0,16},{16,0},{1,17},{17,1},{2,18},{18,2},{3,19},{19,3},{4,20},{20... | collective-permute-start | bytes 786440 | tf_op jit(solution)/shard_map/ppermute | solution.py:13
  169.3 92.0 %copy-start.1 = (f32[4096,128]{1,0:T(8,128)}, f32[4096,128]{1,0:T(8,128)S(1)}, u32[]{:S(2)}) copy-start(f32[4096,128]{1,0:T(8,128)S(1)} %copy.20) | copy-start | bytes 6291460
  180.5 8.3 %collective-permute-start.2 = (f32[20,2,16,128]{3,2,1,0:T(8,128)S(1)}, f32[20,2,16,128]{3,2,1,0:T(8,128)S(1)}, u32[]{:S(2)}, u32[]{:S(2)}) collective-permute-start(f32[20,2,16,128]{3,2,1,0:T(8,128)S(1)} %get-tuple-element.20), channel_id=1, source_target_pairs={{0,4},{4,8},{8,12},{12,0},{1,5},{5,9},{9,13},{13,1},{2,6},{6,10},{... | collective-permute-start | bytes 983048 | tf_op jit(solution)/shard_map/ppermute | solution.py:13
  181.2 8.4 %collective-permute-start.3 = (f32[20,2,16,128]{3,2,1,0:T(8,128)S(1)}, f32[20,2,16,128]{3,2,1,0:T(8,128)S(1)}, u32[]{:S(2)}, u32[]{:S(2)}) collective-permute-start(f32[20,2,16,128]{3,2,1,0:T(8,128)S(1)} %get-tuple-element.21), channel_id=1, source_target_pairs={{4,0},{8,4},{12,8},{0,12},{5,1},{9,5},{13,9},{1,13},{6,2},{10,6},{... | collective-permute-start | bytes 983048 | tf_op jit(solution)/shard_map/ppermute | solution.py:16
  190.8 14.2 %collective-permute-start.4 = (f32[20,20,2,128]{3,2,1,0:T(2,128)S(1)}, f32[20,20,2,128]{3,2,1,0:T(2,128)S(1)}, u32[]{:S(2)}, u32[]{:S(2)}) collective-permute-start(f32[20,20,2,128]{3,2,1,0:T(2,128)S(1)} %get-tuple-element.16), channel_id=1, source_target_pairs={{0,1},{1,2},{2,3},{3,0},{4,5},{5,6},{6,7},{7,4},{8,9},{9,10},{10,1... | collective-permute-start | bytes 1228808 | tf_op jit(solution)/shard_map/ppermute | solution.py:13
  192.0 20.7 %copy-start.3 = (f32[16,16,16]{2,1,0:T(8,128)S(1)}, f32[16,16,16]{2,1,0:T(8,128)}, u32[]{:S(2)}) copy-start(f32[16,16,16]{2,1,0:T(8,128)} %param.3) | copy-start | bytes 49156
  192.0 20.7 %collective-permute-start.5 = (f32[20,20,2,128]{3,2,1,0:T(2,128)S(1)}, f32[20,20,2,128]{3,2,1,0:T(2,128)S(1)}, u32[]{:S(2)}, u32[]{:S(2)}) collective-permute-start(f32[20,20,2,128]{3,2,1,0:T(2,128)S(1)} %get-tuple-element.17), channel_id=1, source_target_pairs={{1,0},{2,1},{3,2},{0,3},{5,4},{6,5},{7,6},{4,7},{9,8},{10,9},{11,1... | collective-permute-start | bytes 1228808 | tf_op jit(solution)/shard_map/ppermute | solution.py:16
  261.3 2.9 %copy-start.4 = (f32[128]{0:T(128)}, f32[128]{0:T(128)S(1)}, u32[]{:S(2)}) copy-start(f32[128]{0:T(128)S(1)} %get-tuple-element.14) | copy-start | bytes 1540
Sparse Core Ops, SparseCore 0:
  14.1 122.0 all-reduce.2
where the time goes:
time: 272 us; the launch traced here: 271 us
  waiting for transfers between devices  161 us (59%)
  blocking collectives  40.1 us (15%)
  other arithmetic  39.7 us (15%)
  between operations  14.1 us (5%)
  starting transfers between devices  7.74 us (3%)
  local copies, waits for them, and re-layouts  6.19 us (2%)
    psum x1, waiting for transfers between devices, local(): correlation = lax.psum(local_correlation, ('gx', 'gy', 'gz')) / total_cells  127 us
    psum x1, blocking collectives, local(): lax.psum((cross, self_applied, self_rotated), ('gx', 'gy', 'gz'))  40.1 us
    ppermute x3, waiting for transfers between devices, extended(): lax.ppermute(lax.slice_in_dim(block, block.shape[dim] - width, None, axis...  20.9 us
    ppermute x3, waiting for transfers between devices, extended(): lax.ppermute(lax.slice_in_dim(block, 0, width, axis=dim), axis, backward)  13.1 us
    another operation x3, other arithmetic, local(): factor = jnp.linalg.cholesky(correlation)  12.4 us
    another operation x2, other arithmetic, local(): lax.linalg.triangular_solve(factor, jnp.eye(bands, dtype=jnp.float32), le...  10.5 us
    reduce_sum x1, other arithmetic, local(): self_applied = jnp.sum(applied * applied, axis=(0, 1, 2))  8.02 us
  transfers between devices with their start and end apart: 7, of which 7 were waited for; matrix products, arithmetic and copies ran while one was open for 1% of the time, Pallas kernels for 0%

commit v1 on v0

--- a/solution.py
+++ b/solution.py
@@ -2,6 +2,11 @@
 import jax.numpy as jnp
 from jax import lax
 from jax.sharding import PartitionSpec as P
+
+
+def summed_here(array, name):
+    parts = lax.all_gather(array, name)
+    return jnp.sum(parts, axis=0)
 
 
 def extended(block, sides, width):
@@ -42,7 +47,7 @@
     local_correlation = lax.dot_general(
         flat, flat, (((0,), (0,)), ((), ())), preferred_element_type=jnp.float32
     )
-    correlation = lax.psum(local_correlation, ("gx", "gy", "gz")) / total_cells
+    correlation = summed_here(local_correlation, ("gx", "gy", "gz")) / total_cells
     factor = jnp.linalg.cholesky(correlation)
     inverse = lax.linalg.triangular_solve(
         factor, jnp.eye(bands, dtype=jnp.float32), left_side=True, lower=True

time: 272 us -> 204 us (0.75)
  waiting for transfers between devices: 161 us -> 94.5 us
    psum x1 -> x0, waiting for transfers between devices: 127 us -> none  [local(): correlation = lax.psum(local_correlation, ('gx', 'gy', 'gz')) / total_cells]
    all_gather x0 -> x1, waiting for transfers between devices: none -> 61.1 us  [summed_here(): parts = lax.all_gather(array, name)]
  transfers between devices with their start and end apart: 7 -> 7, of which waited for: 7 -> 7; matrix products, arithmetic and copies ran while one was open for 1% -> 2% of each run, Pallas kernels for 0% -> 0%
where the time goes in v1:
time: 204 us
  waiting for transfers between devices  94.5 us (46%)
  other arithmetic  39.7 us (19%)
  blocking collectives  39 us (19%)
  between operations  14.1 us (7%)
  starting transfers between devices  7.73 us (4%)
  local copies, waits for them, and re-layouts  6.19 us (3%)
  matrix products  2.48 us (1%)
    all_gather x1, waiting for transfers between devices, summed_here(): parts = lax.all_gather(array, name)  61.1 us
    psum x1, blocking collectives, local(): lax.psum((cross, self_applied, self_rotated), ('gx', 'gy', 'gz'))  39 us
    ppermute x3, waiting for transfers between devices, extended(): lax.ppermute(lax.slice_in_dim(block, block.shape[dim] - width, None, axis...  20.2 us
    ppermute x3, waiting for transfers between devices, extended(): lax.ppermute(lax.slice_in_dim(block, 0, width, axis=dim), axis, backward)  13.2 us
    another operation x3, other arithmetic, local(): factor = jnp.linalg.cholesky(correlation)  12.4 us
    another operation x2, other arithmetic, local(): lax.linalg.triangular_solve(factor, jnp.eye(bands, dtype=jnp.float32), le...  10.5 us
    reduce_sum x1, other arithmetic, local(): self_applied = jnp.sum(applied * applied, axis=(0, 1, 2))  8.02 us
    ppermute x3, starting transfers between devices, extended(): lax.ppermute(lax.slice_in_dim(block, 0, width, axis=dim), axis, backward)  6.49 us
  transfers between devices with their start and end apart: 7, of which 7 were waited for; matrix products, arithmetic and copies ran while one was open for 2% of the time, Pallas kernels for 0%

profile of v1, /device:TPU:0, one launch (start us, length us, event | category | flops | bytes accessed | tf_op | source)
XLA Modules:
  0.0 203.7 jit_solution(8668996563315974278)
XLA Ops:
  7.2 1.2 copy-done
  8.4 1.1 convolution_bitcast_fusion.1
  9.5 61.1 %all-gather.3.cloned.1.call-done = f32[4096,128]{1,0:T(8,128)} async-done(((f32[128,128]{1,0:T(8,128)}), f32[4096,128]{1,0:T(8,128)}) %all-gather.3.cloned.1.call-update) | async-done | bytes 2097168 | tf_op jit(solution)/shard_map/all_gather | solution.py:8
  70.6 1.7 reduce_sum.38
  72.4 11.7 %cholesky.17 = f32[128,128]{1,0:T(8,128)S(1)} custom-call(f32[128,128]{1,0:T(8,128)S(1)} %fusion.25), custom_call_target="Cholesky" | custom-call | tf_op jit(solution)/shard_map/jit(cholesky)/cholesky | solution.py:51
  84.2 0.6 compare_reduce_fusion
  84.8 0.7 fusion.22
  85.5 9.8 %custom-call.6 = f32[1,128,128]{1,2,0:T(8,128)S(1)} custom-call(f32[1,128,128]{2,1,0:T(8,128)S(1)} %fusion.22), custom_call_target="InvertDiagBlocksLowerTriangular" | custom-call | tf_op jit(solution)/shard_map/triangular_solve | solution.py:52
  95.3 0.2 fusion.23
  95.5 1.1 multiply_reduce_fusion
  96.7 1.3 copy-done.2
  98.0 0.8 copy.23
  98.9 0.8 copy.24
  99.7 1.5 collective-permute-start.1
  101.2 0.6 collective-permute-start
  101.7 1.9 copy.22
  103.6 5.4 %collective-permute-done.1 = f32[2,16,16,128]{3,2,1,0:T(8,128)S(1)} collective-permute-done((f32[2,16,16,128]{3,2,1,0:T(8,128)}, f32[2,16,16,128]{3,2,1,0:T(8,128)S(1)}, u32[]{:S(2)}, u32[]{:S(2)}) %collective-permute-start.1) | collective-permute-done | bytes 262176 | tf_op jit(solution)/shard_map/ppermute | solution.py:21
  109.1 5.0 %collective-permute-done = f32[2,16,16,128]{3,2,1,0:T(8,128)} collective-permute-done((f32[2,16,16,128]{3,2,1,0:T(8,128)}, f32[2,16,16,128]{3,2,1,0:T(8,128)}, u32[]{:S(2)}, u32[]{:S(2)}) %collective-permute-start) | collective-permute-done | bytes 262176 | tf_op jit(solution)/shard_map/ppermute | solution.py:18
  114.1 0.8 pad_maximum_fusion.20
  114.9 1.7 collective-permute-start.3
  116.7 6.5 %collective-permute-done.2 = f32[20,2,16,128]{3,2,1,0:T(8,128)S(1)} collective-permute-done((f32[20,2,16,128]{3,2,1,0:T(8,128)S(1)}, f32[20,2,16,128]{3,2,1,0:T(8,128)S(1)}, u32[]{:S(2)}, u32[]{:S(2)}) %collective-permute-start.2) | collective-permute-done | bytes 327712 | tf_op jit(solution)/shard_map/ppermute | solution.py:18
  123.2 0.7 collective-permute-done.3
  123.9 1.3 pad_maximum_fusion.17
  125.2 0.6 collective-permute-start.4
  125.7 3.3 %collective-permute-start.5 = (f32[20,20,2,128]{3,2,1,0:T(2,128)S(1)}, f32[20,20,2,128]{3,2,1,0:T(2,128)S(1)}, u32[]{:S(2)}, u32[]{:S(2)}) collective-permute-start(f32[20,20,2,128]{3,2,1,0:T(2,128)S(1)} %get-tuple-element.17), channel_id=1, source_target_pairs={{1,0},{2,1},{3,2},{0,3},{5,4},{6,5},{7,6},{4,7},{9,8},{10,9},{11,1... | collective-permute-start | bytes 1228808 | tf_op jit(solution)/shard_map/ppermute | solution.py:21
  129.0 1.6 maximum_maximum_fusion
  130.7 8.7 %collective-permute-done.4 = f32[20,20,2,128]{3,2,1,0:T(2,128)S(1)} collective-permute-done((f32[20,20,2,128]{3,2,1,0:T(2,128)S(1)}, f32[20,20,2,128]{3,2,1,0:T(2,128)S(1)}, u32[]{:S(2)}, u32[]{:S(2)}) %collective-permute-start.4) | collective-permute-done | bytes 409632 | tf_op jit(solution)/shard_map/ppermute | solution.py:18
  139.4 7.1 %collective-permute-done.5 = f32[20,20,2,128]{3,2,1,0:T(2,128)S(1)} collective-permute-done((f32[20,20,2,128]{3,2,1,0:T(2,128)S(1)}, f32[20,20,2,128]{3,2,1,0:T(2,128)S(1)}, u32[]{:S(2)}, u32[]{:S(2)}) %collective-permute-start.5) | collective-permute-done | bytes 409632 | tf_op jit(solution)/shard_map/ppermute | solution.py:21
  146.5 8.0 %multiply_reduce_fusion.1 = (f32[128]{0:T(128)S(1)}, f32[128]{0:T(128)S(1)}, f32[16,16,16,128]{3,2,1,0:T(8,128)}) fusion(f32[16,16,16,128]{3,2,1,0:T(8,128)S(1)} %bitcast.29, f32[16,16,16]{2,1,0:T(8,128)S(1)} %copy-done.3, f32[20,20,2,128]{3,2,1,0:T(2,128)S(1)} %collective-permute-done.5, f32[20,2,16,128]{3,2,1,0:T(8,128)S(1)} %collective-permute-done.3, ...), kind=kLoop, calls=%fused_computation.48 | loop fusion | flops 29359872 | bytes 14599168 | tf_op jit(solution)/shard_map/reduce_sum | solution.py:60
  154.5 39.0 %all-reduce = (f32[128]{0:T(128)S(1)}, f32[128]{0:T(128)S(1)}, f32[128]{0:T(128)S(1)}) all-reduce(f32[128]{0:T(128)S(1)} %get-tuple-element.9, f32[128]{0:T(128)S(1)} %get-tuple-element.24, f32[128]{0:T(128)S(1)} %get-tuple-element.8), channel_id=1, replica_groups=mesh['gx'=2,'gy'=4,'gz'=4] {'gx','gy','gz'}, use_global_device_ids=true, to_apply=%region_4.5 | all-reduce | flops 384 | bytes 3072 | tf_op jit(solution)/shard_map/psum | solution.py:62
  193.5 0.5 add_sqrt_fusion
  194.0 2.8 %subtract_convert_fusion = bf16[16,16,16,128]{3,2,1,0:T(8,128)(2,1)} fusion(f32[16,16,16,128]{3,2,1,0:T(8,128)} %get-tuple-element.15, f32[128]{0:T(128)S(1)} %get-tuple-element.14, f32[4096,128]{1,0:T(8,128)S(1)} %copy.22), kind=kLoop, calls=%fused_computation.49 | loop fusion | flops 1572864 | bytes 5243392 | tf_op jit(solution)/shard_map/convert_element_type | solution.py:69
  (15 shorter events, 0.3 us)
Async XLA Ops:
  7.2 1.2 copy-start
  7.2 63.4 %all-gather.3.cloned.1.call-start = ((), (), s32[]{:S(2)}) async-start(), calls=%async_computation | async-start | bytes 2162688 | tf_op jit(solution)/shard_map/all_gather | solution.py:8
  96.7 1.3 copy-start.2
  99.7 9.4 %collective-permute-start.1 = (f32[2,16,16,128]{3,2,1,0:T(8,128)}, f32[2,16,16,128]{3,2,1,0:T(8,128)S(1)}, u32[]{:S(2)}, u32[]{:S(2)}) collective-permute-start(f32[2,16,16,128]{3,2,1,0:T(8,128)} %bitcast.10), channel_id=1, source_target_pairs={{16,0},{0,16},{17,1},{1,17},{18,2},{2,18},{19,3},{3,19},{20,4},{4,... | collective-permute-start | bytes 786440 | tf_op jit(solution)/shard_map/ppermute | solution.py:21
  101.2 12.9 %collective-permute-start = (f32[2,16,16,128]{3,2,1,0:T(8,128)}, f32[2,16,16,128]{3,2,1,0:T(8,128)}, u32[]{:S(2)}, u32[]{:S(2)}) collective-permute-start(f32[2,16,16,128]{3,2,1,0:T(8,128)} %bitcast.9), channel_id=1, source_target_pairs={{0,16},{16,0},{1,17},{17,1},{2,18},{18,2},{3,19},{19,3},{4,20},{20... | collective-permute-start | bytes 786440 | tf_op jit(solution)/shard_map/ppermute | solution.py:18
  103.6 90.4 %copy-start.1 = (f32[4096,128]{1,0:T(8,128)}, f32[4096,128]{1,0:T(8,128)S(1)}, u32[]{:S(2)}) copy-start(f32[4096,128]{1,0:T(8,128)S(1)} %copy.22) | copy-start | bytes 6291460
  114.9 8.3 %collective-permute-start.2 = (f32[20,2,16,128]{3,2,1,0:T(8,128)S(1)}, f32[20,2,16,128]{3,2,1,0:T(8,128)S(1)}, u32[]{:S(2)}, u32[]{:S(2)}) collective-permute-start(f32[20,2,16,128]{3,2,1,0:T(8,128)S(1)} %get-tuple-element.20), channel_id=1, source_target_pairs={{0,4},{4,8},{8,12},{12,0},{1,5},{5,9},{9,13},{13,1},{2,6},{6,10},{... | collective-permute-start | bytes 983048 | tf_op jit(solution)/shard_map/ppermute | solution.py:18
  114.9 8.9 %collective-permute-start.3 = (f32[20,2,16,128]{3,2,1,0:T(8,128)S(1)}, f32[20,2,16,128]{3,2,1,0:T(8,128)S(1)}, u32[]{:S(2)}, u32[]{:S(2)}) collective-permute-start(f32[20,2,16,128]{3,2,1,0:T(8,128)S(1)} %get-tuple-element.21), channel_id=1, source_target_pairs={{4,0},{8,4},{12,8},{0,12},{5,1},{9,5},{13,9},{1,13},{6,2},{10,6},{... | collective-permute-start | bytes 983048 | tf_op jit(solution)/shard_map/ppermute | solution.py:21
  125.2 14.2 %collective-permute-start.4 = (f32[20,20,2,128]{3,2,1,0:T(2,128)S(1)}, f32[20,20,2,128]{3,2,1,0:T(2,128)S(1)}, u32[]{:S(2)}, u32[]{:S(2)}) collective-permute-start(f32[20,20,2,128]{3,2,1,0:T(2,128)S(1)} %get-tuple-element.16), channel_id=1, source_target_pairs={{0,1},{1,2},{2,3},{3,0},{4,5},{5,6},{6,7},{7,4},{8,9},{9,10},{10,1... | collective-permute-start | bytes 1228808 | tf_op jit(solution)/shard_map/ppermute | solution.py:18
  125.7 20.7 %copy-start.3 = (f32[16,16,16]{2,1,0:T(8,128)S(1)}, f32[16,16,16]{2,1,0:T(8,128)}, u32[]{:S(2)}) copy-start(f32[16,16,16]{2,1,0:T(8,128)} %param.3) | copy-start | bytes 49156
  125.7 20.7 %collective-permute-start.5 = (f32[20,20,2,128]{3,2,1,0:T(2,128)S(1)}, f32[20,20,2,128]{3,2,1,0:T(2,128)S(1)}, u32[]{:S(2)}, u32[]{:S(2)}) collective-permute-start(f32[20,20,2,128]{3,2,1,0:T(2,128)S(1)} %get-tuple-element.17), channel_id=1, source_target_pairs={{1,0},{2,1},{3,2},{0,3},{5,4},{6,5},{7,6},{4,7},{9,8},{10,9},{11,1... | collective-permute-start | bytes 1228808 | tf_op jit(solution)/shard_map/ppermute | solution.py:21
  194.0 2.9 %copy-start.4 = (f32[128]{0:T(128)}, f32[128]{0:T(128)S(1)}, u32[]{:S(2)}) copy-start(f32[128]{0:T(128)S(1)} %get-tuple-element.14) | copy-start | bytes 1540
Sparse Core Ops, SparseCore 0:
  11.5 59.0 all-gather.2
